TPU v7x, 32 devices: a whole 2x2x4 slice. The times are simulated.
32 devices in a mesh: prow: 4 (over x, core), pcol: 8 (over z, y).
Axes of the slice: x: 2, y: 2, z: 4, core: 2. Of those that a mesh axis runs over, the one named last changes fastest.
Arguments:
- child_u: bfloat16 [2, 10, 4, 2, 8, 512, 128], P(None, None, 'prow', None, 'pcol'), may hold values from -5 to 5
- child_v: bfloat16 [2, 10, 4, 2, 8, 512, 128], P(None, None, 'prow', None, 'pcol'), may hold values from -5 to 5
- child_rank: int32 [2, 10, 4, 2, 8], P(None, None, 'prow', None, 'pcol'), may hold values from 0 to 128, as said below
- diag_shift: float32 [16, 512], replicated, may hold values from 0.5 to 4
Outputs:
- front_out: float32 [10, 4, 512, 2, 8, 512], P(None, 'prow', None, None, 'pcol')
Inputs may be any that keep to these rules, and one draw needn't show every extreme that they name: `child_rank`: 0 on and above the block diagonal (i <= j); below it 0 where the child has no tile, else from 16 to 128.
All inputs are finite; a program needn't handle non-finite values.
Results may differ from a plain program's by a relative error of at most 0.0003.
Values may be sent and summed in bfloat16 or wider, within the bound.
A program may use at most 320 MiB of HBM per device.

v0:
```python
import jax
import jax.numpy as jnp
from jax import lax
from jax.sharding import PartitionSpec as P

PANELS = 2


def spread(value, axis, root):
    mine = lax.axis_index(axis) == root
    return lax.psum(jnp.where(mine, value, jnp.zeros_like(value)), axis)


def factor_panel(column, panel_index, block_rows, block_cols, own_column, prow_count, pcol_count):
    extent = column.shape[-1]
    pivot_tile = spread(column[panel_index // prow_count], "prow", panel_index % prow_count)
    is_owner = own_column == panel_index % pcol_count
    pivot_tile = jnp.where(is_owner, pivot_tile, jnp.eye(extent, dtype=jnp.float32))
    factor = jnp.linalg.cholesky(pivot_tile)
    solved = lax.linalg.triangular_solve(
        factor, column.reshape(-1, extent), left_side=False, lower=True, transpose_a=True
    ).reshape(column.shape)
    below_mask = (block_rows > panel_index)[:, None, None]
    solved = jnp.where(below_mask, solved, 0.0)
    pivot_diag = jnp.diagonal(factor)
    at_pivot = (block_rows == panel_index)[:, None, None]
    panel_out = jnp.where(
        at_pivot, (factor * pivot_diag[None, :])[None], solved * pivot_diag[None, None, :]
    )
    rounded = solved.astype(jnp.bfloat16)
    received = spread(rounded, "pcol", panel_index % pcol_count)
    picked = jnp.take(received, block_cols // prow_count, axis=0)
    column_rows = spread(picked, "prow", own_column % prow_count)
    return (received, column_rows, panel_out, is_owner)


def trailing(column, received, other_rows):
    return column - jnp.einsum(
        "rab,cb->rac", received, other_rows, preferred_element_type=jnp.float32
    )


def on_device(child_u, child_v, child_rank, diag_shift):
    prow_count = lax.axis_size("prow")
    pcol_count = lax.axis_size("pcol")
    own_row = lax.axis_index("prow")
    own_column = lax.axis_index("pcol")
    rank_grid = child_rank[:, :, 0, :, 0]
    rows_here = rank_grid.shape[1]
    cols_here = rank_grid.shape[2]
    extent = child_u.shape[-2]
    keep_mask = (
        jnp.arange(child_u.shape[-1], dtype=jnp.int32)[None, None, None, :]
        < rank_grid[:, :, :, None]
    ).astype(jnp.bfloat16)
    left_factor = child_u[:, :, 0, :, 0] * keep_mask[:, :, :, None, :]
    right_factor = child_v[:, :, 0, :, 0] * keep_mask[:, :, :, None, :]
    tile_grid = jnp.einsum(
        "crtak,crtbk->rtab", left_factor, right_factor, preferred_element_type=jnp.float32
    )
    row_terms = jnp.einsum(
        "crtak,crtbk->rab", left_factor, left_factor, preferred_element_type=jnp.float32
    )
    column_terms = jnp.einsum(
        "crtak,crtbk->tab", right_factor, right_factor, preferred_element_type=jnp.float32
    )
    kept_rows = cols_here * pcol_count // prow_count
    partial_rows = lax.psum(row_terms[:kept_rows], "pcol")
    spare_rows = jnp.zeros((rows_here - kept_rows, extent, extent), jnp.float32)
    row_sums = jnp.concatenate([partial_rows, spare_rows], axis=0)
    column_sums = lax.psum(column_terms, "prow")
    block_rows = jnp.arange(rows_here, dtype=jnp.int32) * prow_count + own_row
    block_cols = jnp.arange(cols_here, dtype=jnp.int32) * pcol_count + own_column
    slab_total = diag_shift.shape[0]
    select_cols = (block_cols[:, None] == jnp.arange(slab_total, dtype=jnp.int32)[None, :]).astype(
        jnp.float32
    )
    shift_cols = jnp.dot(select_cols, diag_shift, precision=lax.Precision.HIGHEST)
    identity = jnp.eye(extent, dtype=jnp.float32)
    diag_terms = (
        row_sums[:, None]
        + column_sums[None, :]
        + identity[None, None] * shift_cols[None, :, None, :]
    )
    on_diagonal = (block_rows[:, None] == block_cols[None, :])[:, :, None, None]
    tile_grid = tile_grid + jnp.where(on_diagonal, diag_terms, 0.0)
    columns = [tile_grid[:, column_index] for column_index in range(cols_here)]
    results = [jnp.zeros_like(columns[0]) for column_index in range(cols_here)]
    for panel_index in range(PANELS):
        local_col = panel_index // pcol_count
        received, column_rows, panel_out, is_owner = factor_panel(
            columns[local_col],
            panel_index,
            block_rows,
            block_cols,
            own_column,
            prow_count,
            pcol_count,
        )
        results[local_col] = jnp.where(is_owner, panel_out, results[local_col])
        columns = [
            trailing(columns[column_index], received, column_rows[column_index])
            for column_index in range(cols_here)
        ]
    outputs = []
    for column_index in range(cols_here):
        lower_mask = (block_rows >= block_cols[column_index])[:, None, None]
        finished = jnp.where(lower_mask, columns[column_index], 0.0)
        outputs.append(
            jnp.where(block_cols[column_index] < PANELS, results[column_index], finished)
        )
    stacked = jnp.stack(outputs, axis=1)
    return stacked.transpose(0, 2, 1, 3)[:, None, :, :, None, :]


def solution(mesh):
    placed = (
        P(None, None, "prow", None, "pcol", None, None),
        P(None, None, "prow", None, "pcol", None, None),
        P(None, None, "prow", None, "pcol"),
        P(),
    )
    return jax.shard_map(
        on_device,
        mesh=mesh,
        in_specs=placed,
        out_specs=P(None, "prow", None, None, "pcol", None),
        check_vma=False,
    )
```

profile of v0, /device:TPU:0, one launch (start us, length us, event | category | flops | bytes accessed | tf_op | source)
XLA Modules:
  0.0 1351.2 jit_solution(12334410048220816827)
XLA Ops:
  36.5 14.6 %convolution_bitcast_fusion = f32[10,2,512,512]{2,3,0,1:T(8,128)} fusion(bf16[2,10,2,512,128]{4,3,2,1,0:T(8,128)(2,1)} %get-tuple-element.69, bf16[2,10,2,512,128]{4,3,2,1,0:T(8,128)(2,1)} %get-tuple-element.68), kind=kOutput, calls=%fused_computation.35 | convolution fusion | flops 2684354560 | bytes 31457280 | tf_op jit(solution)/shard_map/crtak,crtbk->rtab/dot_general | solution.py:58
  51.1 27.6 %all-reduce.13.cloned.1.call-done = f32[2,512,512]{2,1,0:T(8,128)} async-done(((f32[2,512,512]{2,1,0:T(8,128)}), f32[2,512,512]{2,1,0:T(8,128)}) %all-reduce.13.cloned.1.call-update) | async-done | bytes 2097168 | tf_op jit(solution)/shard_map/psum | solution.py:71
  81.6 157.3 %all-reduce.11.cloned.1.call-done = f32[4,512,512]{2,1,0:T(8,128)} async-done(((f32[4,512,512]{2,1,0:T(8,128)}), f32[4,512,512]{2,1,0:T(8,128)}) %all-reduce.11.cloned.1.call-update) | async-done | bytes 4194320 | tf_op jit(solution)/shard_map/psum | solution.py:68
  251.6 12.6 copy_add_fusion
  293.7 14.7 %all-reduce.15.cloned.1.call-done = f32[512,512]{0,1:T(8,128)} async-done(((f32[512,512]{0,1:T(8,128)}), f32[512,512]{0,1:T(8,128)}) %all-reduce.15.cloned.1.call-update) | async-done | bytes 1048592 | tf_op jit(solution)/shard_map/psum | solution.py:11
  311.6 11.7 cholesky.286
  333.9 11.7 cholesky.305
  356.3 11.7 cholesky.326
  379.2 11.7 cholesky.343
  397.9 11.7 while.4
  409.7 39.9 %custom-call.34 = f32[4,128,128]{1,2,0:T(8,128)} custom-call(f32[4,128,128]{2,1,0:T(8,128)S(1)} %get-tuple-element.22), custom_call_target="InvertDiagBlocksLowerTriangular" | custom-call | tf_op jit(solution)/shard_map/triangular_solve/custom-call.3 | solution.py:20
  475.4 14.6 %fusion.20 = f32[5120,128]{1,0:T(8,128)S(1)} fusion(f32[5120,128]{0,1:T(8,128)S(1)} %fusion.71, f32[5120,128]{0,1:T(8,128)S(1)} %fusion.72, f32[5120,128]{0,1:T(8,128)S(1)} %bitcast.181, f32[5120,512]{1,0:T(8,128)S(1)} %bitcast.191, f32[512,512]{1,0:T(8,128)} %get-tuple-element.198), kind=kOutput, calls=%fused_computation.41 | convolution fusion | flops 3024486400 | bytes 13303808 | tf_op jit(solution)/shard_map/triangular_solve/dot.12 | solution.py:20
  527.8 181.8 %all-reduce.17.cloned.1.call-done = bf16[10,512,512]{1,2,0:T(8,128)(2,1)} async-done(((bf16[10,512,512]{1,2,0:T(8,128)(2,1)}), bf16[10,512,512]{1,2,0:T(8,128)(2,1)}) %all-reduce.17.cloned.1.call-update) | async-done | bytes 5242896 | tf_op jit(solution)/shard_map/psum | solution.py:11
  714.1 35.4 %all-reduce.19.cloned.1.call-done = bf16[2,512,512]{1,2,0:T(8,128)(2,1)} async-done(((bf16[2,512,512]{1,2,0:T(8,128)(2,1)}), bf16[2,512,512]{1,2,0:T(8,128)(2,1)}) %all-reduce.19.cloned.1.call-update) | async-done | bytes 1048592 | tf_op jit(solution)/shard_map/psum | solution.py:11
  775.8 25.4 %all-reduce.21.cloned.1.call-done = f32[512,512]{0,1:T(8,128)} async-done(((f32[512,512]{0,1:T(8,128)}), f32[512,512]{0,1:T(8,128)}) %all-reduce.21.cloned.1.call-update) | async-done | bytes 1048592 | tf_op jit(solution)/shard_map/psum | solution.py:11
  894.0 11.8 while.5
  905.8 39.9 %custom-call.38 = f32[4,128,128]{1,2,0:T(8,128)} custom-call(f32[4,128,128]{2,1,0:T(8,128)S(1)} %get-tuple-element.23), custom_call_target="InvertDiagBlocksLowerTriangular" | custom-call | tf_op jit(solution)/shard_map/triangular_solve/custom-call.3 | solution.py:20
  971.8 14.4 %fusion.17 = f32[5120,128]{1,0:T(8,128)S(1)} fusion(f32[5120,128]{0,1:T(8,128)S(1)} %fusion.65, f32[5120,128]{0,1:T(8,128)S(1)} %fusion.66, f32[5120,128]{0,1:T(8,128)S(1)} %bitcast.184, f32[5120,512]{1,0:T(8,128)S(1)} %bitcast.197, f32[512,512]{1,0:T(8,128)} %get-tuple-element.197), kind=kOutput, calls=%fused_computation.40 | convolution fusion | flops 3024486400 | bytes 13303808 | tf_op jit(solution)/shard_map/triangular_solve/dot.12 | solution.py:20
  1032.1 176.3 %all-reduce.23.cloned.1.call-done = bf16[10,512,512]{1,2,0:T(8,128)(2,1)} async-done(((bf16[10,512,512]{1,2,0:T(8,128)(2,1)}), bf16[10,512,512]{1,2,0:T(8,128)(2,1)}) %all-reduce.23.cloned.1.call-update) | async-done | bytes 5242896 | tf_op jit(solution)/shard_map/psum | solution.py:11
  1226.0 22.1 %all-reduce.25.cloned.1.call-done = bf16[2,512,512]{1,2,0:T(8,128)(2,1)} async-done(((bf16[2,512,512]{1,2,0:T(8,128)(2,1)}), bf16[2,512,512]{1,2,0:T(8,128)(2,1)}) %all-reduce.25.cloned.1.call-update) | async-done | bytes 1048592 | tf_op jit(solution)/shard_map/psum | solution.py:11
  1248.0 18.4 %fusion.4 = f32[10,1,512,512]{2,3,0,1:T(8,128)} fusion(f32[10,512,512]{1,2,0:T(8,128)} %fusion.47, f32[10,2,512,512]{2,3,1,0:T(8,128)} %copy-done.2, pred[10]{0:T(512)(128)(4,1)S(1)} %get-tuple-element.76, pred[]{:T(512)S(6)} %lt.48, bf16[10,512,512]{1,2,0:T(8,128)(2,1)} %all-reduce.23.cloned.1.call-done, bf16[2,512,512]{1,2,0:T(8,128)(2,1)} %all-reduce.25.cloned.1.call-done), kind=kOutput, calls=%fused_computation.15 | convolution fusion | flops 2694840320 | bytes 37224460 | tf_op jit(solution)/shard_map/rab,cb->rac/dot_general | solution.py:38
  1266.4 18.5 %select_bitcast_fusion = f32[10,1,512,512]{2,3,0,1:T(8,128)} fusion(f32[10,512,512]{1,2,0:T(8,128)} %copy-done.3, f32[10,512,512]{1,2,0:T(8,128)} %copy.55, f32[10,512,512]{1,2,0:T(8,128)} %copy.47, f32[512]{0:T(512)S(1)} %gather_fusion.1, f32[512,512]{0,1:T(8,128)S(1)} %copy.56, f32[512]{0:T(512)S(1)} %gather_fusion, f32[512,512]{0,1:T(8,128)S(1)} %copy.52, ...), kind=kOutput, calls=%fused_computation.19 | convolution fusion | flops 2713190400 | bytes 49814020 | tf_op jit(solution)/shard_map/rab,cb->rac/dot_general | solution.py:38
  1284.9 16.2 %maximum_bitcast_fusion = f32[10,1,512,2,1,512]{2,5,0,3,4,1:T(8,128)} fusion(f32[10,1,512,512]{2,3,0,1:T(8,128)} %fusion.4, f32[10,1,512,512]{2,3,0,1:T(8,128)} %select_bitcast_fusion), kind=kLoop, calls=%fused_computation.8 | loop fusion | flops 5242880 | bytes 41943040 | tf_op jit(solution)/shard_map/broadcast_in_dim | solution.py:113
  1301.1 42.9 %copy.66 = f32[10,1,512,2,1,512]{5,4,3,2,1,0:T(1,128)} copy(f32[10,1,512,2,1,512]{2,5,0,3,4,1:T(8,128)} %maximum_bitcast_fusion) | data formatting | bytes 41943040 | tf_op jit(solution)/shard_map/broadcast_in_dim | solution.py:113
  (200 shorter events, 410.6 us)
Async XLA Ops:
  6.5 28.2 %copy-start = (f32[16,512]{1,0:T(8,128)S(1)}, f32[16,512]{1,0:T(8,128)}, u32[]{:S(2)}) copy-start(f32[16,512]{1,0:T(8,128)} %param.12) | copy-start | bytes 98308
  6.5 72.2 %all-reduce.13.cloned.1.call-start = ((), (), s32[]{:S(2)}) async-start(), calls=%async_computation.1 | async-start | bytes 4194304 | tf_op jit(solution)/shard_map/psum | solution.py:71
  24.5 214.4 %all-reduce.11.cloned.1.call-start = ((), (), s32[]{:S(2)}) async-start(), calls=%async_computation | async-start | bytes 8388608 | tf_op jit(solution)/shard_map/psum | solution.py:68
  33.4 275.0 %all-reduce.15.cloned.1.call-start = ((), (), s32[]{:S(2)}) async-start(), calls=%async_computation.2 | async-start | bytes 2097152 | tf_op jit(solution)/shard_map/psum | solution.py:11
  264.3 7.5 copy-start.2
  272.9 436.7 %all-reduce.17.cloned.1.call-start = ((), (), s32[]{:S(2)}) async-start(), calls=%async_computation.3 | async-start | bytes 10485760 | tf_op jit(solution)/shard_map/psum | solution.py:11
  310.1 87.8 %copy-start.13 = (s32[4]{0:T(128)S(1)}, s32[4]{0:T(128)}, u32[]{:S(2)}) copy-start(s32[4]{0:T(128)} %iota_multiply_fusion) | copy-start | bytes 52
  395.2 67.6 %slice-start = ((s8[10485760]{0:T(1024)(128)(4,1)}), s8[2097152]{0:T(1024)(128)(4,1)S(1)}, s32[]{:S(2)}) async-start(s8[10485760]{0:T(1024)(128)(4,1)} %bitcast.188), calls=%async_computation.8 | async-start | bytes 4194304
  449.6 13.3 slice-start.1
  454.0 6.3 copy-start.10
  454.0 8.9 slice-start.2
  508.5 11.3 copy-start.12
  527.7 221.7 %all-reduce.19.cloned.1.call-start = ((), (), s32[]{:S(2)}) async-start(), calls=%async_computation.4 | async-start | bytes 2097152 | tf_op jit(solution)/shard_map/psum | solution.py:11
  714.0 87.2 %all-reduce.21.cloned.1.call-start = ((), (), s32[]{:S(2)}) async-start(), calls=%async_computation.5 | async-start | bytes 2097152 | tf_op jit(solution)/shard_map/psum | solution.py:11
  764.3 444.1 %all-reduce.23.cloned.1.call-start = ((), (), s32[]{:S(2)}) async-start(), calls=%async_computation.6 | async-start | bytes 10485760 | tf_op jit(solution)/shard_map/psum | solution.py:11
  891.0 68.0 %slice-start.3 = ((s8[10485760]{0:T(1024)(128)(4,1)}), s8[2097152]{0:T(1024)(128)(4,1)S(1)}, s32[]{:S(2)}) async-start(s8[10485760]{0:T(1024)(128)(4,1)} %bitcast.194), calls=%async_computation.11 | async-start | bytes 4194304
  945.7 13.3 slice-start.4
  950.1 6.3 copy-start.11
  950.1 8.9 slice-start.5
  1024.0 224.1 %all-reduce.25.cloned.1.call-start = ((), (), s32[]{:S(2)}) async-start(), calls=%async_computation.7 | async-start | bytes 2097152 | tf_op jit(solution)/shard_map/psum | solution.py:11
  1031.6 181.0 %copy-start.8 = (bf16[2,512,512]{1,2,0:T(8,128)(2,1)S(1)}, bf16[2,512,512]{1,2,0:T(8,128)(2,1)}, u32[]{:S(2)}) copy-start(bf16[2,512,512]{1,2,0:T(8,128)(2,1)} %all-reduce.19.cloned.1.call-done) | copy-start | bytes 3145732
  1212.6 8.4 copy-start.4
  1248.0 18.4 %copy-start.9 = (bf16[2,512,512]{1,2,0:T(8,128)(2,1)S(1)}, bf16[2,512,512]{1,2,0:T(8,128)(2,1)}, u32[]{:S(2)}) copy-start(bf16[2,512,512]{1,2,0:T(8,128)(2,1)} %all-reduce.25.cloned.1.call-done) | copy-start | bytes 3145732
  1301.0 42.9 %copy-start.1 = (f32[16,512]{1,0:T(8,128)S(1)}, f32[16,512]{1,0:T(8,128)}, u32[]{:S(2)}) copy-start(f32[16,512]{1,0:T(8,128)} %param.12) | copy-start | bytes 98308
  (4 other events, 12.5 us)
Sparse Core Ops, SparseCore 0:
  24.6 54.0 all-reduce.12
  82.4 156.4 all-reduce.10
  273.1 35.2 all-reduce.14
  527.8 181.7 all-reduce.16
  714.1 35.2 all-reduce.18
  764.4 36.7 all-reduce.20
  1024.1 184.2 all-reduce.22
  1212.7 35.2 all-reduce.24
where the time goes:
time: 1360 us; the launch traced here: 1350 us
  waiting for transfers between devices  641 us (47%)
  other arithmetic  318 us (23%)
  local copies, waits for them, and re-layouts  193 us (14%)
  matrix products  178 us (13%)
  between operations  21.1 us (2%)
    psum x6, waiting for transfers between devices, spread(): return lax.psum(jnp.where(mine, value, jnp.zeros_like(value)), axis)  456 us
    another operation x29, other arithmetic, factor_panel(): factor = jnp.linalg.cholesky(pivot_tile)  159 us
    psum x1, waiting for transfers between devices, on_device(): partial_rows = lax.psum(row_terms[:kept_rows], 'pcol')  157 us
    another operation x7, other arithmetic, factor_panel(): lax.linalg.triangular_solve(factor, column.reshape(-1, extent), left_side...  94.9 us
    another operation x14, matrix products, factor_panel(): lax.linalg.triangular_solve(factor, column.reshape(-1, extent), left_side...  85.9 us
    dot_general x4, matrix products, trailing(): jnp.einsum('rab,cb->rac', received, other_rows, preferred_element_type=jn...  55.1 us
    another operation x29, local copies, waits for them, and re-layouts, factor_panel(): lax.linalg.triangular_solve(factor, column.reshape(-1, extent), left_side...  46.2 us
    broadcast_in_dim x1, local copies, waits for them, and re-layouts, on_device(): return stacked.transpose(0, 2, 1, 3)[:, None, :, :, None, :]  42.9 us
  transfers between devices with their start and end apart: 8, of which 8 were waited for; matrix products, arithmetic and copies ran while one was open for 6% of the time, Pallas kernels for 0%

commit v1 on v0

--- a/solution.py
+++ b/solution.py
@@ -65,7 +65,9 @@
         "crtak,crtbk->tab", right_factor, right_factor, preferred_element_type=jnp.float32
     )
     kept_rows = cols_here * pcol_count // prow_count
-    partial_rows = lax.psum(row_terms[:kept_rows], "pcol")
+    own = row_terms[:kept_rows]
+    shards = lax.all_gather(own, "pcol", axis=0, tiled=False)
+    partial_rows = shards.sum(axis=0)
     spare_rows = jnp.zeros((rows_here - kept_rows, extent, extent), jnp.float32)
     row_sums = jnp.concatenate([partial_rows, spare_rows], axis=0)
     column_sums = lax.psum(column_terms, "prow")

time: 1360 us -> 1820 us (1.34)
  waiting for transfers between devices: 641 us -> 1080 us
    all_gather x0 -> x1, waiting for transfers between devices: none -> 593 us  [on_device(): shards = lax.all_gather(own, 'pcol', axis=0, tiled=False)]
    psum x1 -> x0, waiting for transfers between devices: 157 us -> none  [on_device(): partial_rows = lax.psum(row_terms[:kept_rows], 'pcol')]
  transfers between devices with their start and end apart: 8 -> 8, of which waited for: 8 -> 8; matrix products, arithmetic and copies ran while one was open for 6% -> 5% of each run, Pallas kernels for 0% -> 0%
where the time goes in v1:
time: 1820 us; the launch traced here: 1800 us
  waiting for transfers between devices  1080 us (59%)
  other arithmetic  333 us (18%)
  local copies, waits for them, and re-layouts  193 us (11%)
  matrix products  179 us (10%)
  between operations  22.5 us (1%)
    all_gather x1, waiting for transfers between devices, on_device(): shards = lax.all_gather(own, 'pcol', axis=0, tiled=False)  593 us
    psum x6, waiting for transfers between devices, spread(): return lax.psum(jnp.where(mine, value, jnp.zeros_like(value)), axis)  456 us
    another operation x29, other arithmetic, factor_panel(): factor = jnp.linalg.cholesky(pivot_tile)  159 us
    another operation x7, other arithmetic, factor_panel(): lax.linalg.triangular_solve(factor, column.reshape(-1, extent), left_side...  95.1 us
    another operation x14, matrix products, factor_panel(): lax.linalg.triangular_solve(factor, column.reshape(-1, extent), left_side...  85.9 us
    dot_general x4, matrix products, trailing(): jnp.einsum('rab,cb->rac', received, other_rows, preferred_element_type=jn...  55.1 us
    another operation x29, local copies, waits for them, and re-layouts, factor_panel(): lax.linalg.triangular_solve(factor, column.reshape(-1, extent), left_side...  46 us
    broadcast_in_dim x1, local copies, waits for them, and re-layouts, on_device(): return stacked.transpose(0, 2, 1, 3)[:, None, :, :, None, :]  42.9 us
  transfers between devices with their start and end apart: 8, of which 8 were waited for; matrix products, arithmetic and copies ran while one was open for 5% of the time, Pallas kernels for 0%

profile of v1, /device:TPU:0, one launch (start us, length us, event | category | flops | bytes accessed | tf_op | source)
XLA Modules:
  0.0 1803.4 jit_solution(8560820120586927948)
XLA Ops:
  37.1 15.2 convolution_bitcast_fusion
  52.3 27.2 %all-reduce.10.cloned.1.call-done = f32[2,512,512]{2,1,0:T(8,128)} async-done(((f32[2,512,512]{2,1,0:T(8,128)}), f32[2,512,512]{2,1,0:T(8,128)}) %all-reduce.10.cloned.1.call-update) | async-done | bytes 2097168 | tf_op jit(solution)/shard_map/psum | solution.py:73
  82.4 592.6 %all-gather.3.cloned.1.call-done = f32[32,512,512]{2,1,0:T(8,128)} async-done(((f32[4,512,512]{2,1,0:T(8,128)}), f32[32,512,512]{2,1,0:T(8,128)}) %all-gather.3.cloned.1.call-update) | async-done | bytes 33554448 | tf_op jit(solution)/shard_map/all_gather | solution.py:69
  675.0 15.1 reduce_sum.9
  702.8 12.6 copy_add_fusion
  744.9 15.6 all-reduce.12.cloned.1.call-done
  763.7 11.7 cholesky.286
  786.0 11.7 cholesky.305
  808.4 11.7 cholesky.326
  831.2 11.7 cholesky.343
  850.0 11.9 while.4
  861.9 39.9 %custom-call.34 = f32[4,128,128]{1,2,0:T(8,128)} custom-call(f32[4,128,128]{2,1,0:T(8,128)S(1)} %get-tuple-element.22), custom_call_target="InvertDiagBlocksLowerTriangular" | custom-call | tf_op jit(solution)/shard_map/triangular_solve/custom-call.3 | solution.py:20
  927.7 14.6 fusion.20
  980.2 181.6 %all-reduce.14.cloned.1.call-done = bf16[10,512,512]{1,2,0:T(8,128)(2,1)} async-done(((bf16[10,512,512]{1,2,0:T(8,128)(2,1)}), bf16[10,512,512]{1,2,0:T(8,128)(2,1)}) %all-reduce.14.cloned.1.call-update) | async-done | bytes 5242896 | tf_op jit(solution)/shard_map/psum | solution.py:11
  1166.2 35.4 %all-reduce.16.cloned.1.call-done = bf16[2,512,512]{1,2,0:T(8,128)(2,1)} async-done(((bf16[2,512,512]{1,2,0:T(8,128)(2,1)}), bf16[2,512,512]{1,2,0:T(8,128)(2,1)}) %all-reduce.16.cloned.1.call-update) | async-done | bytes 1048592 | tf_op jit(solution)/shard_map/psum | solution.py:11
  1227.9 25.4 %all-reduce.18.cloned.1.call-done = f32[512,512]{0,1:T(8,128)} async-done(((f32[512,512]{0,1:T(8,128)}), f32[512,512]{0,1:T(8,128)}) %all-reduce.18.cloned.1.call-update) | async-done | bytes 1048592 | tf_op jit(solution)/shard_map/psum | solution.py:11
  1357.5 39.9 %custom-call.38 = f32[4,128,128]{1,2,0:T(8,128)} custom-call(f32[4,128,128]{2,1,0:T(8,128)S(1)} %get-tuple-element.23), custom_call_target="InvertDiagBlocksLowerTriangular" | custom-call | tf_op jit(solution)/shard_map/triangular_solve/custom-call.3 | solution.py:20
  1423.5 14.4 fusion.17
  1484.4 175.6 %all-reduce.20.cloned.1.call-done = bf16[10,512,512]{1,2,0:T(8,128)(2,1)} async-done(((bf16[10,512,512]{1,2,0:T(8,128)(2,1)}), bf16[10,512,512]{1,2,0:T(8,128)(2,1)}) %all-reduce.20.cloned.1.call-update) | async-done | bytes 5242896 | tf_op jit(solution)/shard_map/psum | solution.py:11
  1677.7 22.1 %all-reduce.22.cloned.1.call-done = bf16[2,512,512]{1,2,0:T(8,128)(2,1)} async-done(((bf16[2,512,512]{1,2,0:T(8,128)(2,1)}), bf16[2,512,512]{1,2,0:T(8,128)(2,1)}) %all-reduce.22.cloned.1.call-update) | async-done | bytes 1048592 | tf_op jit(solution)/shard_map/psum | solution.py:11
  1699.7 18.4 %fusion.4 = f32[10,1,512,512]{2,3,0,1:T(8,128)} fusion(f32[10,512,512]{1,2,0:T(8,128)} %fusion.47, f32[10,2,512,512]{2,3,1,0:T(8,128)} %copy-done.2, pred[10]{0:T(512)(128)(4,1)S(1)} %get-tuple-element.76, pred[]{:T(512)S(6)} %lt.48, bf16[10,512,512]{1,2,0:T(8,128)(2,1)} %all-reduce.20.cloned.1.call-done, bf16[2,512,512]{1,2,0:T(8,128)(2,1)} %all-reduce.22.cloned.1.call-done), kind=kOutput, calls=%fused_computation.15 | convolution fusion | flops 2694840320 | bytes 37224460 | tf_op jit(solution)/shard_map/rab,cb->rac/dot_general | solution.py:38
  1718.1 18.5 %select_bitcast_fusion = f32[10,1,512,512]{2,3,0,1:T(8,128)} fusion(f32[10,512,512]{1,2,0:T(8,128)} %copy-done.3, f32[10,512,512]{1,2,0:T(8,128)} %copy.83, f32[10,512,512]{1,2,0:T(8,128)} %copy.75, f32[512]{0:T(512)S(1)} %gather_fusion.1, f32[512,512]{0,1:T(8,128)S(1)} %copy.84, f32[512]{0:T(512)S(1)} %gather_fusion, f32[512,512]{0,1:T(8,128)S(1)} %copy.80, ...), kind=kOutput, calls=%fused_computation.19 | convolution fusion | flops 2713190400 | bytes 49814020 | tf_op jit(solution)/shard_map/rab,cb->rac/dot_general | solution.py:38
  1736.6 16.2 maximum_bitcast_fusion
  1752.7 42.9 %copy.94 = f32[10,1,512,2,1,512]{5,4,3,2,1,0:T(1,128)} copy(f32[10,1,512,2,1,512]{2,5,0,3,4,1:T(8,128)} %maximum_bitcast_fusion) | data formatting | bytes 41943040 | tf_op jit(solution)/shard_map/broadcast_in_dim | solution.py:115
  (203 shorter events, 422.0 us)
Async XLA Ops:
  7.4 28.0 %copy-start = (f32[16,512]{1,0:T(8,128)S(1)}, f32[16,512]{1,0:T(8,128)}, u32[]{:S(2)}) copy-start(f32[16,512]{1,0:T(8,128)} %param.12) | copy-start | bytes 98308
  7.4 72.2 %all-reduce.10.cloned.1.call-start = ((), (), s32[]{:S(2)}) async-start(), calls=%async_computation | async-start | bytes 4194304 | tf_op jit(solution)/shard_map/psum | solution.py:73
  25.3 649.7 %all-gather.3.cloned.1.call-start = ((), (), s32[]{:S(2)}) async-start(), calls=%async_computation.7 | async-start | bytes 37748736 | tf_op jit(solution)/shard_map/all_gather | solution.py:69
  34.5 726.0 %all-reduce.12.cloned.1.call-start = ((), (), s32[]{:S(2)}) async-start(), calls=%async_computation.1 | async-start | bytes 2097152 | tf_op jit(solution)/shard_map/psum | solution.py:11
  715.4 7.5 copy-start.2
  724.1 437.7 %all-reduce.14.cloned.1.call-start = ((), (), s32[]{:S(2)}) async-start(), calls=%async_computation.2 | async-start | bytes 10485760 | tf_op jit(solution)/shard_map/psum | solution.py:11
  762.2 87.8 %copy-start.14 = (s32[4]{0:T(128)S(1)}, s32[4]{0:T(128)}, u32[]{:S(2)}) copy-start(s32[4]{0:T(128)} %iota_multiply_fusion) | copy-start | bytes 52
  843.0 4.4 copy-start.6
  847.4 67.7 %slice-start = ((s8[10485760]{0:T(1024)(128)(4,1)}), s8[2097152]{0:T(1024)(128)(4,1)S(1)}, s32[]{:S(2)}) async-start(s8[10485760]{0:T(1024)(128)(4,1)} %bitcast.189), calls=%async_computation.8 | async-start | bytes 4194304
  901.9 13.3 slice-start.1
  906.3 6.3 copy-start.10
  906.3 8.9 slice-start.2
  980.0 221.5 %all-reduce.16.cloned.1.call-start = ((), (), s32[]{:S(2)}) async-start(), calls=%async_computation.3 | async-start | bytes 2097152 | tf_op jit(solution)/shard_map/psum | solution.py:11
  1166.1 87.2 %all-reduce.18.cloned.1.call-start = ((), (), s32[]{:S(2)}) async-start(), calls=%async_computation.4 | async-start | bytes 2097152 | tf_op jit(solution)/shard_map/psum | solution.py:11
  1216.4 443.6 %all-reduce.20.cloned.1.call-start = ((), (), s32[]{:S(2)}) async-start(), calls=%async_computation.5 | async-start | bytes 10485760 | tf_op jit(solution)/shard_map/psum | solution.py:11
  1343.1 67.6 %slice-start.3 = ((s8[10485760]{0:T(1024)(128)(4,1)}), s8[2097152]{0:T(1024)(128)(4,1)S(1)}, s32[]{:S(2)}) async-start(s8[10485760]{0:T(1024)(128)(4,1)} %bitcast.195), calls=%async_computation.11 | async-start | bytes 4194304
  1397.5 13.2 slice-start.4
  1401.9 6.3 copy-start.11
  1401.9 8.8 slice-start.5
  1475.8 223.9 %all-reduce.22.cloned.1.call-start = ((), (), s32[]{:S(2)}) async-start(), calls=%async_computation.6 | async-start | bytes 2097152 | tf_op jit(solution)/shard_map/psum | solution.py:11
  1483.9 180.3 %copy-start.8 = (bf16[2,512,512]{1,2,0:T(8,128)(2,1)S(1)}, bf16[2,512,512]{1,2,0:T(8,128)(2,1)}, u32[]{:S(2)}) copy-start(bf16[2,512,512]{1,2,0:T(8,128)(2,1)} %all-reduce.16.cloned.1.call-done) | copy-start | bytes 3145732
  1664.3 8.4 copy-start.4
  1699.7 18.4 %copy-start.9 = (bf16[2,512,512]{1,2,0:T(8,128)(2,1)S(1)}, bf16[2,512,512]{1,2,0:T(8,128)(2,1)}, u32[]{:S(2)}) copy-start(bf16[2,512,512]{1,2,0:T(8,128)(2,1)} %all-reduce.22.cloned.1.call-done) | copy-start | bytes 3145732
  1752.7 42.9 %copy-start.1 = (f32[16,512]{1,0:T(8,128)S(1)}, f32[16,512]{1,0:T(8,128)}, u32[]{:S(2)}) copy-start(f32[16,512]{1,0:T(8,128)} %param.12) | copy-start | bytes 98308
  (5 other events, 9.7 us)
Sparse Core Ops, SparseCore 0:
  25.4 54.0 all-reduce.9
  724.2 36.2 all-reduce.11
  1166.2 35.2 all-reduce.15
  1216.5 36.7 all-reduce.17
  1664.4 35.2 all-reduce.21
Sparse Core Ops, SparseCore 1:
  34.6 640.4 all-gather.2
  980.1 181.6 all-reduce.13
  1475.9 184.1 all-reduce.19
